TPU v7x, 32 devices: a whole 2x2x4 slice. The times are simulated.
32 devices in a mesh: src: 16 (over z, y, core), tgt: 2 (over x).
Axes of the slice: x: 2, y: 2, z: 4, core: 2. Of those that a mesh axis runs over, the one named last changes fastest.
Arguments:
- src_emb: bfloat16 [8192, 1024], P('src', 'tgt'), may hold values from -16 to 16
- tgt_emb: bfloat16 [8192, 1024], P('tgt', 'src'), may hold values from -16 to 16
- src_ids: int32 [8192], P('src'), may hold values from 0 to 4095
- tgt_ids: int32 [8192], P('tgt'), may hold values from 0 to 4095
Outputs:
- margin: float32 [8192, 8192], P('src', 'tgt')
All inputs are finite; a program needn't handle non-finite values.
Results may differ from a plain program's by a relative error of at most 0.004.
Values may be sent and summed in bfloat16 or wider, within the bound.
A program may use at most 64 MiB of HBM per device.

v0:
```python
import jax
import jax.numpy as jnp
from jax import lax
from jax.sharding import PartitionSpec as P

epsilon = 1e-06
excluded_score = -2.0


def unit_rows(embedded):
    values = embedded.astype(jnp.float32)
    scale = jnp.sqrt(jnp.sum(values * values, axis=1, keepdims=True) + epsilon)
    return (values / scale).astype(jnp.bfloat16)


def best_four(values, axis=1):
    upper = jnp.float32(jnp.inf)
    levels = []
    counts = []
    for step in range(4):
        below = jnp.where(values < upper, values, -jnp.inf)
        level = jnp.max(below, axis=axis, keepdims=True)
        counts.append(jnp.sum((values == level).astype(jnp.int32), axis=axis))
        level = jnp.squeeze(level, axis=axis)
        levels.append(level)
        upper = jnp.expand_dims(level, axis)
    entries = []
    for place in range(4):
        chosen = levels[3]
        running = counts[0] + counts[1] + counts[2]
        for level_index in (2, 1, 0):
            chosen = jnp.where(running > place, levels[level_index], chosen)
            if level_index > 0:
                running = running - counts[level_index]
        entries.append(chosen)
    return jnp.stack(entries, axis=-1)


def merge_lists(first, second):
    return best_four(jnp.concatenate([first, second], axis=1))


def body(src_emb, tgt_emb, src_ids, tgt_ids):
    src_whole = lax.all_gather(src_emb, "tgt", axis=1, tiled=True)
    tgt_whole = lax.all_gather(tgt_emb, "src", axis=1, tiled=True)
    src_unit = unit_rows(src_whole)
    tgt_unit = unit_rows(tgt_whole)
    src_rows = src_unit.shape[0]
    tgt_rows = tgt_unit.shape[0]
    width = src_unit.shape[1]
    block_rows = min(512, src_rows)
    blocks = src_rows // block_rows
    src_blocks = src_unit.reshape(blocks, block_rows, width)
    id_blocks = src_ids.reshape(blocks, block_rows)

    def cosines(rows, row_ids):
        scores = lax.dot_general(
            rows, tgt_unit, (((1,), (1,)), ((), ())), preferred_element_type=jnp.float32
        )
        same = row_ids[:, None] == tgt_ids[None, :]
        return (jnp.where(same, jnp.float32(excluded_score), scores), same)

    def first_pass(column_best, pieces):
        rows, row_ids = pieces
        scores, same = cosines(rows, row_ids)
        row_best = best_four(scores, 1)
        merged = merge_lists(column_best, best_four(scores, 0))
        return (merged, row_best)

    start = jnp.full((tgt_rows, 4), excluded_score, jnp.float32)
    column_best, row_best = lax.scan(first_pass, start, (src_blocks, id_blocks))
    row_best = row_best.reshape(src_rows, 4)
    row_final = best_four(lax.all_gather(row_best, "tgt", axis=1, tiled=True))
    column_final = best_four(
        lax.all_gather(column_best.astype(jnp.bfloat16), "src", axis=1, tiled=True).astype(
            column_best.dtype
        )
    )
    knn_src = jnp.mean(row_final, axis=-1).reshape(blocks, block_rows)
    knn_tgt = jnp.mean(column_final, axis=-1)

    def second_pass(pieces):
        rows, row_ids, row_knn = pieces
        scores, same = cosines(rows, row_ids)
        ratio = scores / (0.5 * (row_knn[:, None] + knn_tgt[None, :]))
        return jnp.where(same, jnp.float32(0.0), ratio)

    margin = lax.map(second_pass, (src_blocks, id_blocks, knn_src))
    return margin.reshape(src_rows, tgt_rows)


def solution(mesh):
    return jax.shard_map(
        body,
        mesh=mesh,
        in_specs=(P("src", "tgt"), P("tgt", "src"), P("src"), P("tgt")),
        out_specs=P("src", "tgt"),
        check_vma=False,
    )
```

profile of v0, /device:TPU:0, one launch (start us, length us, event | category | flops | bytes accessed | tf_op | source)
XLA Modules:
  0.0 173.5 jit_solution(16949459775546920627)
XLA Ops:
  6.5 0.0 copy-start.3
  6.5 0.0 copy-start.4
  6.5 0.0 all-gather.5.cloned.1.call-start
  6.5 0.7 all-gather.5.cloned.1.call-update
  7.3 0.0 all-gather.7.cloned.1.call-start
  7.3 0.7 all-gather.7.cloned.1.call-update
  8.0 24.9 %all-gather.5.cloned.1.call-done = bf16[512,1024]{1,0:T(8,128)(2,1)} async-done(((bf16[512,512]{1,0:T(8,128)(2,1)}), bf16[512,1024]{1,0:T(8,128)(2,1)}) %all-gather.5.cloned.1.call-update) | async-done | bytes 1048592 | tf_op jit(solution)/shard_map/all_gather | solution.py:44
  32.9 0.0 copy-start.2
  32.9 1.6 fusion.14
  34.5 74.9 %all-gather.7.cloned.1.call-done = bf16[4096,1024]{0,1:T(8,128)(2,1)} async-done(((bf16[4096,64]{0,1:T(8,128)(2,1)}), bf16[4096,1024]{0,1:T(8,128)(2,1)}) %all-gather.7.cloned.1.call-update) | async-done | bytes 8388624 | tf_op jit(solution)/shard_map/all_gather | solution.py:45
  109.4 0.0 copy-start.1
  109.4 5.2 %fusion = f32[4096]{0:T(1024)S(1)} fusion(bf16[4096,1024]{0,1:T(8,128)(2,1)} %all-gather.7.cloned.1.call-done), kind=kLoop, calls=%fused_computation.9 | loop fusion | flops 12578816 | bytes 8404992 | tf_op jit(solution)/shard_map/reduce_sum | solution.py:12
  114.6 0.0 copy-done.3
  114.7 0.0 copy-done.4
  114.7 0.0 copy-done.2
  114.7 0.5 copy-done.1
  115.2 5.2 %fusion.11 = (f32[512]{0:T(512)S(1)}, f32[512,4096]{1,0:T(8,128)S(1)}) fusion(bf16[4096,1024]{0,1:T(8,128)(2,1)S(1)} %copy-done.1, f32[4096]{0:T(1024)S(1)} %add_sqrt_fusion, bf16[512,1024]{1,0:T(8,128)(2,1)S(1)} %copy-done.2, f32[512]{0:T(512)S(1)} %add_sqrt_fusion.1, s32[4096]{0:T(1024)S(1)} %copy-done.3, s32[512]{0:T(512)S(1)} %copy-done.4), kind=kOutput, calls=%fused_computation.27 | convolution fusion | flops 4319608320 | bytes 17864704 | tf_op jit(solution)/shard_map/while/body/eval_jaxpr/dot_general | solution.py:57
  120.4 0.0 copy-start
  120.4 1.0 fusion.2
  121.3 1.0 fusion.3
  122.3 2.1 %fusion.4 = (f32[512]{0:T(512)S(1)}, f32[4096]{0:T(1024)S(1)}) fusion(f32[512,4096]{1,0:T(8,128)S(1)} %get-tuple-element.86, f32[512]{0:T(512)S(1)} %fusion.3), kind=kLoop, calls=%fused_computation.15 | loop fusion | flops 12578304 | bytes 8409088 | tf_op jit(solution)/shard_map/while/body/eval_jaxpr/reduce_max | solution.py:22
  124.4 1.0 fusion.5
  125.4 1.0 fusion.6
  126.4 1.0 fusion.7
  127.4 0.0 copy-done
  127.4 5.7 %convert_reduce_fusion.3 = (s32[512]{0:T(512)S(1)}, s32[4096]{0:T(1024)S(1)}, s32[4096]{0:T(1024)S(1)}, s32[512]{0:T(512)S(1)}, s32[512]{0:T(512)S(1)}, /*index=5*/s32[4096]{0:T(1024)S(1)}) fusion(f32[512,4096]{1,0:T(8,128)S(1)} %get-tuple-element.86, f32[512]{0:T(512)S(1)} %fusion.3, f32[4096]{0:T(1024)S(1)} %get-tuple-element.47, f32[4096]{0:T(1024)S(1)} %fusion.6, ...), kind=kLoop, calls=%fused_computation.22 | loop fusion | flops 37734912 | bytes 8499200 | tf_op jit(solution)/shard_map/while/body/eval_jaxpr/reduce_sum | solution.py:23
  133.2 4.4 %all-gather = f32[2,4,512]{2,1,0:T(4,128)S(1)} all-gather(f32[1,4,512]{2,1,0:T(4,128)S(1)} %maximum_bitcast_fusion.1), channel_id=1, replica_groups=mesh['src'=16,'tgt'=2] {'tgt'}, dimensions={0}, use_global_device_ids=true | all-gather | bytes 24576 | tf_op jit(solution)/shard_map/all_gather | solution.py:73
  137.8 0.1 concatenate.4
  138.1 0.1 fusion.25
  138.1 0.1 convert_reduce_fusion.9
  138.4 0.1 maximum_bitcast_fusion
  138.5 20.4 %all-gather.1 = bf16[16,4,4096]{2,1,0:T(4,128)(2,1)S(1)} all-gather(bf16[1,4,4096]{2,1,0:T(4,128)(2,1)S(1)} %maximum_bitcast_fusion), channel_id=1, replica_groups=mesh['src'=16,'tgt'=2] {'src'}, dimensions={0}, use_global_device_ids=true | all-gather | bytes 557056 | tf_op jit(solution)/shard_map/all_gather | solution.py:75
  158.9 0.1 reshape.932
  159.0 0.1 fusion.17
  159.1 0.1 fusion.18
  159.3 0.1 fusion.19
  159.4 0.1 fusion.20
  159.5 0.4 convert_reduce_fusion.7
  160.0 6.7 %compare_select_fusion.7 = f32[512,4096]{1,0:T(8,128)} fusion(f32[512,4096]{1,0:T(8,128)} %copy-done, f32[4096]{0:T(1024)S(1)} %add_multiply_fusion, f32[512]{0:T(512)S(1)} %add_multiply_fusion.1, s32[4096]{0:T(1024)S(1)} %copy-done.3, s32[512]{0:T(512)S(1)} %copy-done.4), kind=kLoop, calls=%fused_computation.11 | loop fusion | flops 10485760 | bytes 16814080 | tf_op jit(solution)/shard_map/while/body/eval_jaxpr/jit(_where)/select_n | solution.py:86
  (25 shorter events, 0.5 us)
Async XLA Ops:
  6.5 108.1 %copy-start.3 = (s32[4096]{0:T(1024)S(1)}, s32[4096]{0:T(1024)}, u32[]{:S(2)}) copy-start(s32[4096]{0:T(1024)} %param.7) | copy-start | bytes 49156
  6.5 108.1 %copy-start.4 = (s32[512]{0:T(512)S(1)}, s32[512]{0:T(512)}, u32[]{:S(2)}) copy-start(s32[512]{0:T(512)} %param.6) | copy-start | bytes 6148
  6.5 26.4 %all-gather.5.cloned.1.call-start = ((), (), s32[]{:S(2)}) async-start(), calls=%async_computation | async-start | bytes 1572864 | tf_op jit(solution)/shard_map/all_gather | solution.py:44
  7.3 102.1 %all-gather.7.cloned.1.call-start = ((), (), s32[]{:S(2)}) async-start(), calls=%async_computation.1 | async-start | bytes 8912896 | tf_op jit(solution)/shard_map/all_gather | solution.py:45
  32.9 81.8 %copy-start.2 = (bf16[512,1024]{1,0:T(8,128)(2,1)S(1)}, bf16[512,1024]{1,0:T(8,128)(2,1)}, u32[]{:S(2)}) copy-start(bf16[512,1024]{1,0:T(8,128)(2,1)} %all-gather.5.cloned.1.call-done) | copy-start | bytes 3145732
  109.4 5.8 %copy-start.1 = (bf16[4096,1024]{0,1:T(8,128)(2,1)S(1)}, bf16[4096,1024]{0,1:T(8,128)(2,1)}, u32[]{:S(2)}) copy-start(bf16[4096,1024]{0,1:T(8,128)(2,1)} %all-gather.7.cloned.1.call-done) | copy-start | bytes 25165828
  120.4 7.1 %copy-start = (f32[512,4096]{1,0:T(8,128)}, f32[512,4096]{1,0:T(8,128)S(1)}, u32[]{:S(2)}) copy-start(f32[512,4096]{1,0:T(8,128)S(1)} %get-tuple-element.86) | copy-start | bytes 25165828
Sparse Core Ops, SparseCore 0:
  8.9 23.9 all-gather.4
  35.1 74.2 all-gather.6
where the time goes:
time: 174 us; the launch traced here: 173 us
  waiting for transfers between devices  101 us (58%)
  other arithmetic  27.9 us (16%)
  blocking collectives  24.8 us (14%)
  between operations  13.6 us (8%)
  matrix products  5.18 us (3%)
    all_gather x1, waiting for transfers between devices, body(): tgt_whole = lax.all_gather(tgt_emb, 'src', axis=1, tiled=True)  74.9 us
    all_gather x1, waiting for transfers between devices, body(): src_whole = lax.all_gather(src_emb, 'tgt', axis=1, tiled=True)  24.9 us
    all_gather x1, blocking collectives, body(): lax.all_gather(column_best.astype(jnp.bfloat16), 'src', axis=1, tiled=True)  20.4 us
    reduce_max x18, other arithmetic, best_four(): level = jnp.max(below, axis=axis, keepdims=True)  7.88 us
    reduce_sum x2, other arithmetic, unit_rows(): scale = jnp.sqrt(jnp.sum(values * values, axis=1, keepdims=True) + epsilon)  6.81 us
    select_n x1, other arithmetic, second_pass(): return jnp.where(same, jnp.float32(0.0), ratio)  6.66 us
    reduce_sum x4, other arithmetic, best_four(): counts.append(jnp.sum((values == level).astype(jnp.int32), axis=axis))  6.27 us
    dot_general x1, matrix products, cosines(): lax.dot_general(rows, tgt_unit, (((1,), (1,)), ((), ())), preferred_eleme...  5.18 us
  transfers between devices with their start and end apart: 2, of which 2 were waited for; matrix products, arithmetic and copies ran while one was open for 1% of the time, Pallas kernels for 0%

commit v1 on v0

v1 whole, which is shorter than its diff:
```python
import functools

import jax
import jax.numpy as jnp
from jax import lax
from jax.experimental import pallas as pl
from jax.experimental.pallas import tpu as pltpu
from jax.sharding import PartitionSpec as P

epsilon = 1e-06
excluded_score = -2.0
MESH = pl.DeviceIdType.MESH
CHUNK = 512


def insert(best, value):
    out = []
    for level in best[:-1]:
        out.append(jnp.maximum(level, value))
        value = jnp.minimum(level, value)
    out.append(jnp.maximum(best[-1], value))
    return tuple(out)


def merge(first, second):
    c = [jnp.maximum(first[k], second[3 - k]) for k in range(4)]
    a, b = jnp.maximum(c[0], c[2]), jnp.maximum(c[1], c[3])
    d, e = jnp.minimum(c[0], c[2]), jnp.minimum(c[1], c[3])
    return (jnp.maximum(a, b), jnp.minimum(a, b), jnp.maximum(d, e), jnp.minimum(d, e))


def fold_sublanes(best):
    for shift in (4, 2, 1):
        best = merge(best, tuple(pltpu.roll(level, shift, 0) for level in best))
    return best


def stacked(best):
    row = lax.broadcasted_iota(jnp.int32, best[0].shape, 0)
    low = jnp.full(best[0].shape, -jnp.inf, jnp.float32)
    for k in range(3, -1, -1):
        low = jnp.where(row == k, best[k], low)
    return low


def lowest(shape):
    return tuple(jnp.full(shape, -jnp.inf, jnp.float32) for _ in range(4))


def kernel(dims, x_ref, a_ref, sid_ref, tid_ref, s_out, kt_out, ks_out, g, a_whole, a_unit, b_unit, sbuf, rowbest,
           colbuf, colin, ktown, ktin, rowbuf, rowin, zrecv, zsend, yrecv, ysend, crecv, csend, arecv, asend, rrecv,
           rsend, krecv, ksend, mrecv, msend, lsem, osem):
    ns, nt, nz, chunks, cw, feats = dims
    s = lax.axis_index("src")
    t = lax.axis_index("tgt")
    z, y, c = s // 4, (s // 2) % 2, s % 2
    zy = s // 2
    right = (s + 4, t)
    left = (s - 4, t)
    over = (zy + 1 - 2 * y) * 2 + c
    rows = a_unit.shape[0]
    part = a_ref.shape[1]
    ow = colbuf.shape[2]
    has_right, has_left = z + 1 < nz, z >= 1

    def remote(src, dst, send, recv, where):
        return pltpu.make_async_remote_copy(
            src_ref=src, dst_ref=dst, send_sem=send, recv_sem=recv, device_id=where, device_id_type=MESH
        )

    local = pltpu.make_async_copy(x_ref, g.at[:, zy, c], lsem.at[0])
    local.start()
    acols = pl.ds(pl.multiple_of(t * part, part), part)
    local_a = pltpu.make_async_copy(a_ref, a_whole.at[:, acols], lsem.at[1])
    local_a.start()

    barrier = pltpu.get_barrier_semaphore()
    for k in range(1, ns):
        pl.semaphore_signal(barrier, inc=1, device_id=(lax.rem(s + k, ns), t), device_id_type=MESH)
    for k in range(1, nt):
        pl.semaphore_signal(barrier, inc=1, device_id=(s, lax.rem(t + k, nt)), device_id_type=MESH)
    pl.semaphore_wait(barrier, ns - 1 + nt - 1)

    def to_right(j, zp, own):
        ref = g.at[j, zp * 2 + y, c]
        return remote(x_ref.at[j] if own else ref, ref, zsend.at[0, j, zp], zrecv.at[j, zp], right)

    def to_left(j, zp, own):
        ref = g.at[j, zp * 2 + y, c]
        return remote(x_ref.at[j] if own else ref, ref, zsend.at[1, j, zp], zrecv.at[j, zp], left)

    def to_over(j, zp, own):
        ref = g.at[j, zp * 2 + y, c]
        return remote(x_ref.at[j] if own else ref, ref, ysend.at[j, zp], yrecv.at[j, zp], (over, t))

    def from_over(j, zp):
        ref = g.at[j, zp * 2 + 1 - y, c]
        return remote(ref, ref, ysend.at[j, zp], yrecv.at[j, zp], (over, t))

    def to_core(j):
        ref = g.at[j, :, c]
        return remote(ref, ref, csend.at[j], crecv.at[j], (s + 1 - 2 * c, t))

    def from_core(j):
        ref = g.at[j, :, 1 - c]
        return remote(ref, ref, csend.at[j], crecv.at[j], (s + 1 - 2 * c, t))

    def start_own(j):
        @pl.when(has_right)
        def _():
            to_right(j, z, True).start()

        @pl.when(has_left)
        def _():
            to_left(j, z, True).start()

    def to_tgt(k):
        return remote(a_ref, a_whole.at[:, acols], asend.at[k], arecv.at[t], (s, lax.rem(t + k, nt)))

    ahead = min(2, chunks)
    for j in range(ahead):
        start_own(j)
    for k in range(1, nt):
        to_tgt(k).start()
    local.wait()

    def normalize_sources():
        local_a.wait()
        for k in range(1, nt):
            other = lax.rem(t + k, nt)
            cols = pl.ds(pl.multiple_of(other * part, part), part)
            remote(a_ref, a_whole.at[:, cols], asend.at[k], arecv.at[other], (s, other)).wait_recv()
        block = 16

        def step(r, carry):
            at = pl.ds(pl.multiple_of(r * block, block), block)
            v = a_whole[at, :].astype(jnp.float32)
            scale = jnp.sqrt(jnp.sum(v * v, axis=1, keepdims=True) + epsilon)
            a_unit[at, :] = (v / scale).astype(jnp.bfloat16)
            return carry

        lax.fori_loop(0, rows // block, step, 0)
        for k in range(4):
            rowbest[k] = jnp.full(rowbest.shape[1:], -jnp.inf, jnp.float32)

    def out_copy(j):
        at = pl.ds(pl.multiple_of(j * cw, cw), cw)
        return pltpu.make_async_copy(sbuf.at[j % 2], s_out.at[:, at], osem.at[j % 2])

    def compute(j):
        def squares(k, acc):
            v = g[j, k // 2, k % 2].astype(jnp.float32)
            return acc + jnp.sum((v * v).reshape(feats // 8, 8, cw), axis=0)

        acc = lax.fori_loop(0, ns, squares, jnp.zeros((8, cw), jnp.float32))
        inverse = 1.0 / jnp.sqrt(jnp.sum(acc, axis=0, keepdims=True) + epsilon)

        def scale(k, carry):
            v = g[j, k // 2, k % 2].astype(jnp.float32)
            b_unit[pl.ds(pl.multiple_of(k * feats, feats), feats), :] = (v * inverse).astype(jnp.bfloat16)
            return carry

        lax.fori_loop(0, ns, scale, 0)

        @pl.when(j >= 2)
        def _():
            out_copy(j - 2).wait()

        slot = j % 2
        sbuf[slot] = jnp.dot(a_unit[...], b_unit[...], preferred_element_type=jnp.float32)
        tids = tid_ref[j]

        def group(r, best):
            at = pl.ds(pl.multiple_of(r * 8, 8), 8)
            ids = sid_ref[at, :]
            row = tuple(rowbest[k, at, :] for k in range(4))
            pieces = []
            for q in range(cw // 128):
                lanes = pl.ds(q * 128, 128)
                v = sbuf[slot, at, lanes]
                v = jnp.where(ids == tids[:, q * 128 : (q + 1) * 128], jnp.float32(excluded_score), v)
                row = insert(row, v)
                sbuf[slot, at, lanes] = v
                pieces.append(v)
            for k in range(4):
                rowbest[k, at, :] = row[k]
            return tuple(insert(best[q], pieces[q]) for q in range(cw // 128))

        best = lax.fori_loop(0, rows // 8, group, tuple(lowest((8, 128)) for _ in range(cw // 128)), unroll=2)
        out_copy(j).start()
        per = ow // 128
        for q in range(cw // 128):
            colbuf[j * (cw // ow) + q // per, :, (q % per) * 128 : (q % per + 1) * 128] = stacked(fold_sublanes(best[q]))

    def tick(i, carry):
        @pl.when(i + ahead < chunks)
        def _():
            start_own(i + ahead)

        @pl.when(i < chunks)
        def _():
            to_over(i, z, True).start()
            for d in range(1, nz):
                @pl.when(z - d >= 0)
                def _():
                    to_right(i, z - d, False).wait_recv()

                    @pl.when(has_right)
                    def _():
                        to_right(i, z - d, False).start()

                    to_over(i, z - d, False).start()

                @pl.when(z + d < nz)
                def _():
                    to_left(i, z + d, False).wait_recv()

                    @pl.when(has_left)
                    def _():
                        to_left(i, z + d, False).start()

                    to_over(i, z + d, False).start()

        @pl.when(jnp.logical_and(i >= 1, i <= chunks))
        def _():
            for zp in range(nz):
                from_over(i - 1, zp).wait_recv()
            to_core(i - 1).start()

        @pl.when(i == 2)
        def _():
            normalize_sources()

        @pl.when(i >= 2)
        def _():
            from_core(i - 2).wait_recv()
            compute(i - 2)

        return carry

    lax.fori_loop(0, chunks + 2, tick, 0)

    def col_copy(k):
        other = lax.rem(s + k, ns)
        return remote(colbuf.at[other], colin.at[s], ksend.at[k], krecv.at[s], (other, t))

    for k in range(1, ns):
        col_copy(k).start()
    colin[s] = colbuf[s]


    best = lowest((8, rows))
    for k in range(4):
        flat = rowbest[k].T
        for q in range(128 // 8):
            best = insert(best, flat[q * 8 : (q + 1) * 8, :])
    rowbuf[...] = stacked(fold_sublanes(best))
    rowin[t] = rowbuf[...]

    def row_copy(k):
        other = lax.rem(t + k, nt)
        return remote(rowbuf, rowin.at[t], rsend.at[k], rrecv.at[t], (s, other))

    for k in range(1, nt):
        row_copy(k).start()

    for k in range(1, ns):
        other = lax.rem(s + k, ns)
        remote(colbuf.at[0], colin.at[other], ksend.at[k], krecv.at[other], (other, t)).wait_recv()
    best = lowest((8, ow))
    for p in range(ns):
        best = insert(best, colin[p])
    best = fold_sublanes(best)
    ktown[...] = (best[0] + best[1] + best[2] + best[3]) * 0.25

    def mean_copy(k):
        other = lax.rem(s + k, ns)
        return remote(ktown, ktin.at[s], msend.at[k], mrecv.at[s], (other, t))

    for k in range(1, ns):
        mean_copy(k).start()
    ktin[s] = ktown[...]

    for k in range(1, nt):
        other = lax.rem(t + k, nt)
        remote(rowbuf, rowin.at[other], rsend.at[k], rrecv.at[other], (s, other)).wait_recv()
    best = lowest((8, rows))
    for p in range(nt):
        best = insert(best, rowin[p])
    best = fold_sublanes(best)
    ks_out[...] = (best[0] + best[1] + best[2] + best[3]) * 0.25

    def drain(j, carry):
        for zp in range(nz):
            @pl.when(jnp.logical_and(has_right, zp <= z))
            def _():
                to_right(j, zp, False).wait_send()

            @pl.when(jnp.logical_and(has_left, zp >= z))
            def _():
                to_left(j, zp, False).wait_send()

            to_over(j, zp, False).wait_send()
        to_core(j).wait_send()
        return carry

    lax.fori_loop(0, chunks, drain, 0)
    for j in range(max(0, chunks - 2), chunks):
        out_copy(j).wait()
    for k in range(1, nt):
        to_tgt(k).wait_send()
        row_copy(k).wait_send()
    for k in range(1, ns):
        col_copy(k).wait_send()
        mean_copy(k).wait_send()
    for k in range(1, ns):
        other = lax.rem(s + k, ns)
        remote(ktown, ktin.at[other], msend.at[k], mrecv.at[other], (other, t)).wait_recv()
    kt_out[...] = ktin[...]


def body(ns, nt, src_emb, tgt_emb, src_ids, tgt_ids):
    rows, part = src_emb.shape
    cols, feats = tgt_emb.shape
    width = part * nt
    nz = ns // 4
    cw = min(CHUNK, cols)
    chunks = cols // cw
    ow = cols // ns
    x = tgt_emb.reshape(chunks, cw, feats).transpose(0, 2, 1)
    sid = jnp.broadcast_to(src_ids[:, None], (rows, 128))
    tid = jnp.broadcast_to(tgt_ids.reshape(chunks, 1, cw), (chunks, 8, cw))
    f32, bf16 = jnp.float32, jnp.bfloat16
    dma = pltpu.SemaphoreType.DMA
    vmem = pl.BlockSpec(memory_space=pltpu.VMEM)
    scores, kt, ks = pl.pallas_call(
        functools.partial(kernel, (ns, nt, nz, chunks, cw, feats)),
        out_shape=(
            jax.ShapeDtypeStruct((rows, cols), f32),
            jax.ShapeDtypeStruct((ns, 8, ow), f32),
            jax.ShapeDtypeStruct((8, rows), f32),
        ),
        in_specs=[vmem] * 4,
        out_specs=(pl.BlockSpec(memory_space=pl.ANY), vmem, vmem),
        scratch_shapes=[
            pltpu.VMEM((chunks, ns // 2, 2, feats, cw), bf16),
            pltpu.VMEM((rows, width), bf16),
            pltpu.VMEM((rows, width), bf16),
            pltpu.VMEM((width, cw), bf16),
            pltpu.VMEM((2, rows, cw), f32),
            pltpu.VMEM((4, rows, 128), f32),
            pltpu.VMEM((ns, 8, ow), f32),
            pltpu.VMEM((ns, 8, ow), f32),
            pltpu.VMEM((8, ow), f32),
            pltpu.VMEM((ns, 8, ow), f32),
            pltpu.VMEM((8, rows), f32),
            pltpu.VMEM((nt, 8, rows), f32),
            dma((chunks, nz)),
            dma((2, chunks, nz)),
            dma((chunks, nz)),
            dma((chunks, nz)),
            dma((chunks,)),
            dma((chunks,)),
            dma((nt,)),
            dma((nt,)),
            dma((nt,)),
            dma((nt,)),
            dma((ns,)),
            dma((ns,)),
            dma((ns,)),
            dma((ns,)),
            dma((2,)),
            dma((2,)),
        ],
        compiler_params=pltpu.CompilerParams(
            collective_id=0, has_side_effects=True, vmem_limit_bytes=32 * 2**20
        ),
    )(x, src_emb, sid, tid)
    knn_src = ks[0]
    knn_tgt = kt[:, 0, :].reshape(cols)
    ratio = scores / (0.5 * (knn_src[:, None] + knn_tgt[None, :]))
    return jnp.where(src_ids[:, None] == tgt_ids[None, :], jnp.float32(0.0), ratio)


def solution(mesh):
    return jax.shard_map(
        functools.partial(body, mesh.shape["src"], mesh.shape["tgt"]),
        mesh=mesh,
        in_specs=(P("src", "tgt"), P("tgt", "src"), P("src"), P("tgt")),
        out_specs=P("src", "tgt"),
        check_vma=False,
    )
```

time: 174 us -> 89.4 us (0.51)
  waiting for transfers between devices: 101 us -> 0 us
  Pallas kernels: 0 us -> 80.2 us
  blocking collectives: 24.8 us -> 0 us
  other arithmetic: 27.9 us -> 5.14 us
  between operations: 13.6 us -> 0.05 us
  matrix products: 5.18 us -> 0 us
  local copies, waits for them, and re-layouts: 0.78 us -> 3.67 us
    all_gather x2 -> x0, waiting for transfers between devices: 99.8 us -> none  [the longest x1 74.9 us: body(): tgt_whole = lax.all_gather(tgt_emb, 'src', axis=1, tiled=True)]
    pallas_call x0 -> x1, Pallas kernels: none -> 80.2 us  [body(): pl.pallas_call(functools.partial(kernel, (ns, nt, nz, chunks, cw, feats))...]
    all_gather x2 -> x0, blocking collectives: 24.8 us -> none  [the longest x1 20.4 us: body(): lax.all_gather(column_best.astype(jnp.bfloat16), 'src', axis=1, tiled=True)]
    reduce_sum x6 -> x0, other arithmetic: 13.1 us -> none  [the longest x2 6.81 us: unit_rows(): scale = jnp.sqrt(jnp.sum(values * values, axis=1, keepdims=True) + epsilon)]
    reduce_max x18 -> x0, other arithmetic: 7.88 us -> none  [best_four(): level = jnp.max(below, axis=axis, keepdims=True)]
    dot_general x1 -> x0, matrix products: 5.18 us -> none  [cosines(): lax.dot_general(rows, tgt_unit, (((1,), (1,)), ((), ())), preferred_eleme...]
    select_n x5 -> x1, other arithmetic: 6.7 us -> 5.14 us  [body(): jnp.where(src_ids[:, None] == tgt_ids[None, :], jnp.float32(0.0), ratio)]
  transfers between devices with their start and end apart: 2 -> 0, of which waited for: 2 -> 0; matrix products, arithmetic and copies ran while one was open for 1% -> 0% of each run, Pallas kernels for 0% -> 0%
where the time goes in v1:
time: 89.4 us; the launch traced here: 89.1 us
  Pallas kernels  80.2 us (90%)
  other arithmetic  5.14 us (6%)
  local copies, waits for them, and re-layouts  3.67 us (4%)
    pallas_call x1, Pallas kernels, body(): pl.pallas_call(functools.partial(kernel, (ns, nt, nz, chunks, cw, feats))...  80.2 us
    select_n x1, other arithmetic, body(): jnp.where(src_ids[:, None] == tgt_ids[None, :], jnp.float32(0.0), ratio)  5.14 us

profile of v1, /device:TPU:0, one launch (start us, length us, event | category | flops | bytes accessed | tf_op | source)
XLA Modules:
  0.0 89.1 jit_solution(18292993994416552794)
XLA Ops:
  0.0 0.7 broadcast_in_dim.21
  0.7 0.8 broadcast_in_dim.20.sid_ref
  1.5 1.1 %copy.8 = bf16[8,8,8,512]{3,2,0,1:T(8,128)(2,1)S(1)} copy(bf16[8,8,8,512]{3,2,1,0:T(8,128)(2,1)} %bitcast.10) | data formatting | bytes 1048576 | tf_op jit(solution)/shard_map/reshape | solution.py:330
  2.6 0.0 copy-start
  2.7 1.0 %copy-done = bf16[512,512]{1,0:T(8,128)(2,1)S(1)} copy-done((bf16[512,512]{1,0:T(8,128)(2,1)S(1)}, bf16[512,512]{1,0:T(8,128)(2,1)}, u32[]{:S(2)}) %copy-start) | copy-done | bytes 524312
  3.7 80.2 %shard_map.46 = (f32[512,4096]{1,0:T(8,128)S(1)}, f32[16,8,256]{2,1,0:T(8,128)S(1)}, f32[8,512]{1,0:T(8,128)S(1)}) custom-call(bf16[8,64,512]{2,1,0:T(8,128)(2,1)S(1)} %bitcast.9, bf16[512,512]{1,0:T(8,128)(2,1)S(1)} %copy-done, s32[512,128]{1,0:T(8,128)S(1)} %broadcast_in_dim.20.sid_ref, s32[8,8,512]{2,1,0:T(8,128)S(1)} %broadcast_in_dim.22.tid_ref), custom_call_target="tpu_custom_call" | custom-call | tf_op jit(solution)/shard_map/pallas_call | solution.py:336
  84.0 5.1 %divide_select_fusion = f32[512,4096]{1,0:T(8,128)} fusion(f32[512,4096]{1,0:T(8,128)S(1)} %get-tuple-element.8, f32[4096]{0:T(1024)S(1)} %bitcast.11, f32[512]{0:T(512)S(1)} %bitcast.12, s32[4096]{0:T(1024)} %param.7, s32[512]{0:T(512)} %param.6), kind=kLoop, calls=%fused_computation | loop fusion | flops 10485760 | bytes 16814080 | tf_op jit(solution)/shard_map/jit(_where)/select_n | solution.py:382
  (3 shorter events, 0.0 us)
Async XLA Ops:
  2.6 1.0 %copy-start = (bf16[512,512]{1,0:T(8,128)(2,1)S(1)}, bf16[512,512]{1,0:T(8,128)(2,1)}, u32[]{:S(2)}) copy-start(bf16[512,512]{1,0:T(8,128)(2,1)} %a_ref.1) | copy-start | bytes 1572868

commit v2 on v1

--- a/solution.py
+++ b/solution.py
@@ -11,6 +11,9 @@
 excluded_score = -2.0
 MESH = pl.DeviceIdType.MESH
 CHUNK = 512
+EVERY = 8
+OVER_AHEAD = 4
+LAG = 1
 
 
 def insert(best, value):
@@ -47,17 +50,17 @@
     return tuple(jnp.full(shape, -jnp.inf, jnp.float32) for _ in range(4))
 
 
-def kernel(dims, x_ref, a_ref, sid_ref, tid_ref, s_out, kt_out, ks_out, g, a_whole, a_unit, b_unit, sbuf, rowbest,
+def kernel(dims, x_ref, a_ref, sid_ref, tid_ref, s_out, kt_out, ks_out, sids, g, a_whole, a_unit, b_unit, sbuf, rowbest,
            colbuf, colin, ktown, ktin, rowbuf, rowin, zrecv, zsend, yrecv, ysend, crecv, csend, arecv, asend, rrecv,
            rsend, krecv, ksend, mrecv, msend, lsem, osem):
     ns, nt, nz, chunks, cw, feats = dims
     s = lax.axis_index("src")
     t = lax.axis_index("tgt")
     z, y, c = s // 4, (s // 2) % 2, s % 2
-    zy = s // 2
     right = (s + 4, t)
     left = (s - 4, t)
-    over = (zy + 1 - 2 * y) * 2 + c
+    over = (z * 4 + (1 - y) * 2 + c, t)
+    core = (s + 1 - 2 * c, t)
     rows = a_unit.shape[0]
     part = a_ref.shape[1]
     ow = colbuf.shape[2]
@@ -68,61 +71,85 @@
             src_ref=src, dst_ref=dst, send_sem=send, recv_sem=recv, device_id=where, device_id_type=MESH
         )
 
-    local = pltpu.make_async_copy(x_ref, g.at[:, zy, c], lsem.at[0])
-    local.start()
+    def chunk_cols(j):
+        return pl.ds(pl.multiple_of(j * cw, cw), cw)
+
+    local = [
+        pltpu.make_async_copy(x_ref.at[:, j * cw : (j + 1) * cw], g.at[j, z, y, c], lsem.at[1 + j]) for j in range(chunks)
+    ]
+    for copy in local:
+        copy.start()
     acols = pl.ds(pl.multiple_of(t * part, part), part)
-    local_a = pltpu.make_async_copy(a_ref, a_whole.at[:, acols], lsem.at[1])
+    local_a = pltpu.make_async_copy(a_ref, a_whole.at[:, acols], lsem.at[0])
     local_a.start()
 
     barrier = pltpu.get_barrier_semaphore()
-    for k in range(1, ns):
-        pl.semaphore_signal(barrier, inc=1, device_id=(lax.rem(s + k, ns), t), device_id_type=MESH)
+
+    @pl.when(has_right)
+    def _():
+        pl.semaphore_signal(barrier, inc=1, device_id=right, device_id_type=MESH)
+
+    @pl.when(has_left)
+    def _():
+        pl.semaphore_signal(barrier, inc=1, device_id=left, device_id_type=MESH)
+
+    pl.semaphore_signal(barrier, inc=1, device_id=over, device_id_type=MESH)
+    pl.semaphore_signal(barrier, inc=1, device_id=core, device_id_type=MESH)
     for k in range(1, nt):
         pl.semaphore_signal(barrier, inc=1, device_id=(s, lax.rem(t + k, nt)), device_id_type=MESH)
-    pl.semaphore_wait(barrier, ns - 1 + nt - 1)
-
-    def to_right(j, zp, own):
-        ref = g.at[j, zp * 2 + y, c]
-        return remote(x_ref.at[j] if own else ref, ref, zsend.at[0, j, zp], zrecv.at[j, zp], right)
-
-    def to_left(j, zp, own):
-        ref = g.at[j, zp * 2 + y, c]
-        return remote(x_ref.at[j] if own else ref, ref, zsend.at[1, j, zp], zrecv.at[j, zp], left)
-
-    def to_over(j, zp, own):
-        ref = g.at[j, zp * 2 + y, c]
-        return remote(x_ref.at[j] if own else ref, ref, ysend.at[j, zp], yrecv.at[j, zp], (over, t))
+    pl.semaphore_wait(barrier, 1 + nt + has_right.astype(jnp.int32) + has_left.astype(jnp.int32))
+
+    def y_first(j):
+        return lax.rem(j, EVERY) == EVERY - 1
+
+    def to_right(j, zp, yy):
+        ref = g.at[j, zp, yy, c]
+        return remote(ref, ref, zsend.at[0, j, zp, yy], zrecv.at[j, zp, yy], right)
+
+    def to_left(j, zp, yy):
+        ref = g.at[j, zp, yy, c]
+        return remote(ref, ref, zsend.at[1, j, zp, yy], zrecv.at[j, zp, yy], left)
+
+    def to_over(j, zp):
+        ref = g.at[j, zp, y, c]
+        return remote(ref, ref, ysend.at[j, zp], yrecv.at[j, zp], over)
 
     def from_over(j, zp):
-        ref = g.at[j, zp * 2 + 1 - y, c]
-        return remote(ref, ref, ysend.at[j, zp], yrecv.at[j, zp], (over, t))
-
-    def to_core(j):
-        ref = g.at[j, :, c]
-        return remote(ref, ref, csend.at[j], crecv.at[j], (s + 1 - 2 * c, t))
-
-    def from_core(j):
-        ref = g.at[j, :, 1 - c]
-        return remote(ref, ref, csend.at[j], crecv.at[j], (s + 1 - 2 * c, t))
-
-    def start_own(j):
+        ref = g.at[j, zp, 1 - y, c]
+        return remote(ref, ref, ysend.at[j, zp], yrecv.at[j, zp], over)
+
+    def to_core(j, yy):
+        ref = g.at[j, :, yy, c]
+        return remote(ref, ref, csend.at[j, yy], crecv.at[j, yy], core)
+
+    def from_core(j, yy):
+        ref = g.at[j, :, yy, 1 - c]
+        return remote(ref, ref, csend.at[j, yy], crecv.at[j, yy], core)
+
+    def start_z(j, yy):
         @pl.when(has_right)
         def _():
-            to_right(j, z, True).start()
+            to_right(j, z, yy).start()
 
         @pl.when(has_left)
         def _():
-            to_left(j, z, True).start()
+            to_left(j, z, yy).start()
 
     def to_tgt(k):
         return remote(a_ref, a_whole.at[:, acols], asend.at[k], arecv.at[t], (s, lax.rem(t + k, nt)))
 
     ahead = min(2, chunks)
+    behind = nz - 1 + LAG
+    for copy in local:
+        copy.wait()
     for j in range(ahead):
-        start_own(j)
+        start_z(j, y)
+    for j in range(chunks):
+        if j < OVER_AHEAD or j % EVERY == EVERY - 1:
+            to_over(j, z).start()
     for k in range(1, nt):
         to_tgt(k).start()
-    local.wait()
+    sids[...] = jnp.broadcast_to(sid_ref[...], (128, rows)).T
 
     def normalize_sources():
         local_a.wait()
@@ -144,19 +171,18 @@
             rowbest[k] = jnp.full(rowbest.shape[1:], -jnp.inf, jnp.float32)
 
     def out_copy(j):
-        at = pl.ds(pl.multiple_of(j * cw, cw), cw)
-        return pltpu.make_async_copy(sbuf.at[j % 2], s_out.at[:, at], osem.at[j % 2])
+        return pltpu.make_async_copy(sbuf.at[j % 2], s_out.at[:, chunk_cols(j)], osem.at[j % 2])
 
     def compute(j):
         def squares(k, acc):
-            v = g[j, k // 2, k % 2].astype(jnp.float32)
+            v = g[j, k // 4, (k // 2) % 2, k % 2].astype(jnp.float32)
             return acc + jnp.sum((v * v).reshape(feats // 8, 8, cw), axis=0)
 
         acc = lax.fori_loop(0, ns, squares, jnp.zeros((8, cw), jnp.float32))
         inverse = 1.0 / jnp.sqrt(jnp.sum(acc, axis=0, keepdims=True) + epsilon)
 
         def scale(k, carry):
-            v = g[j, k // 2, k % 2].astype(jnp.float32)
+            v = g[j, k // 4, (k // 2) % 2, k % 2].astype(jnp.float32)
             b_unit[pl.ds(pl.multiple_of(k * feats, feats), feats), :] = (v * inverse).astype(jnp.bfloat16)
             return carry
 
@@ -168,11 +194,11 @@
 
         slot = j % 2
         sbuf[slot] = jnp.dot(a_unit[...], b_unit[...], preferred_element_type=jnp.float32)
-        tids = tid_ref[j]
+        tids = jnp.broadcast_to(tid_ref[:, chunk_cols(j)], (8, cw))
 
         def group(r, best):
             at = pl.ds(pl.multiple_of(r * 8, 8), 8)
-            ids = sid_ref[at, :]
+            ids = sids[at, :]
             row = tuple(rowbest[k, at, :] for k in range(4))
             pieces = []
             for q in range(cw // 128):
@@ -192,53 +218,86 @@
         for q in range(cw // 128):
             colbuf[j * (cw // ow) + q // per, :, (q % per) * 128 : (q % per + 1) * 128] = stacked(fold_sublanes(best[q]))
 
+    def within(j):
+        return jnp.logical_and(j >= 0, j < chunks)
+
+    def stage(j, d, first):
+        both = (y, 1 - y) if first else (y,)
+
+        @pl.when(z - d >= 0)
+        def _():
+            for yy in both:
+                to_right(j, z - d, yy).wait_recv()
+
+                @pl.when(has_right)
+                def _():
+                    to_right(j, z - d, yy).start()
+
+            if not first:
+                to_over(j, z - d).start()
+
+        @pl.when(z + d < nz)
+        def _():
+            for yy in both:
+                to_left(j, z + d, yy).wait_recv()
+
+                @pl.when(has_left)
+                def _():
+                    to_left(j, z + d, yy).start()
+
+            if not first:
+                to_over(j, z + d).start()
+
+        if d == nz - 1:
+            for yy in both:
+                to_core(j, yy).start()
+
     def tick(i, carry):
         @pl.when(i + ahead < chunks)
         def _():
-            start_own(i + ahead)
-
-        @pl.when(i < chunks)
-        def _():
-            to_over(i, z, True).start()
-            for d in range(1, nz):
-                @pl.when(z - d >= 0)
-                def _():
-                    to_right(i, z - d, False).wait_recv()
-
-                    @pl.when(has_right)
-                    def _():
-                        to_right(i, z - d, False).start()
-
-                    to_over(i, z - d, False).start()
-
-                @pl.when(z + d < nz)
-                def _():
-                    to_left(i, z + d, False).wait_recv()
-
-                    @pl.when(has_left)
-                    def _():
-                        to_left(i, z + d, False).start()
-
-                    to_over(i, z + d, False).start()
-
-        @pl.when(jnp.logical_and(i >= 1, i <= chunks))
+            start_z(i + ahead, y)
+
+            @pl.when(y_first(i + ahead))
+            def _():
+                from_over(i + ahead, z).wait_recv()
+                start_z(i + ahead, 1 - y)
+
+        @pl.when(jnp.logical_and(i + OVER_AHEAD < chunks, jnp.logical_not(y_first(i + OVER_AHEAD))))
+        def _():
+            to_over(i + OVER_AHEAD, z).start()
+
+        for d in range(1, nz):
+            j = i - d + 1
+
+            @pl.when(jnp.logical_and(within(j), jnp.logical_not(y_first(j))))
+            def _():
+                stage(j, d, False)
+
+            @pl.when(jnp.logical_and(within(j), y_first(j)))
+            def _():
+                stage(j, d, True)
+
+        jy = i - nz + 1
+
+        @pl.when(jnp.logical_and(within(jy), jnp.logical_not(y_first(jy))))
         def _():
             for zp in range(nz):
-                from_over(i - 1, zp).wait_recv()
-            to_core(i - 1).start()
-
-        @pl.when(i == 2)
+                from_over(jy, zp).wait_recv()
+            to_core(jy, 1 - y).start()
+
+        @pl.when(i == behind)
         def _():
             normalize_sources()
 
-        @pl.when(i >= 2)
-        def _():
-            from_core(i - 2).wait_recv()
-            compute(i - 2)
+        @pl.when(i >= behind)
+        def _():
+            for yy in range(2):
+                from_core(i - behind, yy).wait_recv()
+            compute(i - behind)
 
         return carry
 
-    lax.fori_loop(0, chunks + 2, tick, 0)
+    lax.fori_loop(0, chunks + behind, tick, 0)
 
     def col_copy(k):
         other = lax.rem(s + k, ns)
@@ -291,17 +350,31 @@
     ks_out[...] = (best[0] + best[1] + best[2] + best[3]) * 0.25
 
     def drain(j, carry):
-        for zp in range(nz):
+        def drain_z(zp, yy):
             @pl.when(jnp.logical_and(has_right, zp <= z))
             def _():
-                to_right(j, zp, False).wait_send()
+                to_right(j, zp, yy).wait_send()
 
             @pl.when(jnp.logical_and(has_left, zp >= z))
             def _():
-                to_left(j, zp, False).wait_send()
-
-            to_over(j, zp, False).wait_send()
-        to_core(j).wait_send()
+                to_left(j, zp, yy).wait_send()
+
+        for zp in range(nz):
+            drain_z(zp, y)
+
+        @pl.when(y_first(j))
+        def _():
+            for zp in range(nz):
+                drain_z(zp, 1 - y)
+            to_over(j, z).wait_send()
+
+        @pl.when(jnp.logical_not(y_first(j)))
+        def _():
+            for zp in range(nz):
+                to_over(j, zp).wait_send()
+
+        for yy in range(2):
+            to_core(j, yy).wait_send()
         return carry
 
     lax.fori_loop(0, chunks, drain, 0)
@@ -327,11 +400,9 @@
     cw = min(CHUNK, cols)
     chunks = cols // cw
     ow = cols // ns
-    x = tgt_emb.reshape(chunks, cw, feats).transpose(0, 2, 1)
-    sid = jnp.broadcast_to(src_ids[:, None], (rows, 128))
-    tid = jnp.broadcast_to(tgt_ids.reshape(chunks, 1, cw), (chunks, 8, cw))
     f32, bf16 = jnp.float32, jnp.bfloat16
     dma = pltpu.SemaphoreType.DMA
+    hbm = pl.BlockSpec(memory_space=pl.ANY)
     vmem = pl.BlockSpec(memory_space=pltpu.VMEM)
     scores, kt, ks = pl.pallas_call(
         functools.partial(kernel, (ns, nt, nz, chunks, cw, feats)),
@@ -340,10 +411,11 @@
             jax.ShapeDtypeStruct((ns, 8, ow), f32),
             jax.ShapeDtypeStruct((8, rows), f32),
         ),
-        in_specs=[vmem] * 4,
-        out_specs=(pl.BlockSpec(memory_space=pl.ANY), vmem, vmem),
+        in_specs=[hbm, hbm, vmem, vmem],
+        out_specs=(hbm, vmem, vmem),
         scratch_shapes=[
-            pltpu.VMEM((chunks, ns // 2, 2, feats, cw), bf16),
+            pltpu.VMEM((rows, 128), jnp.int32),
+            pltpu.VMEM((chunks, nz, 2, 2, feats, cw), bf16),
             pltpu.VMEM((rows, width), bf16),
             pltpu.VMEM((rows, width), bf16),
             pltpu.VMEM((width, cw), bf16),
@@ -355,12 +427,12 @@
             pltpu.VMEM((ns, 8, ow), f32),
             pltpu.VMEM((8, rows), f32),
             pltpu.VMEM((nt, 8, rows), f32),
-            dma((chunks, nz)),
-            dma((2, chunks, nz)),
+            dma((chunks, nz, 2)),
+            dma((2, chunks, nz, 2)),
             dma((chunks, nz)),
             dma((chunks, nz)),
-            dma((chunks,)),
-            dma((chunks,)),
+            dma((chunks, 2)),
+            dma((chunks, 2)),
             dma((nt,)),
             dma((nt,)),
             dma((nt,)),
@@ -369,13 +441,13 @@
             dma((ns,)),
             dma((ns,)),
             dma((ns,)),
-            dma((2,)),
+            dma((1 + chunks,)),
             dma((2,)),
         ],
         compiler_params=pltpu.CompilerParams(
             collective_id=0, has_side_effects=True, vmem_limit_bytes=32 * 2**20
         ),
-    )(x, src_emb, sid, tid)
+    )(tgt_emb.T, src_emb, src_ids.reshape(1, rows), tgt_ids.reshape(1, cols))
     knn_src = ks[0]
     knn_tgt = kt[:, 0, :].reshape(cols)
     ratio = scores / (0.5 * (knn_src[:, None] + knn_tgt[None, :]))

time: 89.4 us -> 82 us (0.917)
  Pallas kernels: 80.2 us -> 73.7 us
    pallas_call x1, Pallas kernels: 80.2 us -> 73.7 us  [body(): pl.pallas_call(functools.partial(kernel, (ns, nt, nz, chunks, cw, feats))...]
    unnamed x2 -> x8, local copies, waits for them, and re-layouts: 1.04 us -> 3.48 us
    broadcast_in_dim x3 -> x0, local copies, waits for them, and re-layouts: 1.54 us -> none  [the longest x1 0.8 us: body(): sid = jnp.broadcast_to(src_ids[:, None], (rows, 128))]
    reshape x1 -> x0, local copies, waits for them, and re-layouts: 1.09 us -> none  [body(): x = tgt_emb.reshape(chunks, cw, feats).transpose(0, 2, 1)]
where the time goes in v2:
time: 82 us; the launch traced here: 81.7 us
  Pallas kernels  73.7 us (90%)
  other arithmetic  4.45 us (5%)
  local copies, waits for them, and re-layouts  3.49 us (4%)
    pallas_call x1, Pallas kernels, body(): pl.pallas_call(functools.partial(kernel, (ns, nt, nz, chunks, cw, feats))...  73.7 us
    select_n x1, other arithmetic, body(): jnp.where(src_ids[:, None] == tgt_ids[None, :], jnp.float32(0.0), ratio)  4.45 us
    unnamed x8, local copies, waits for them, and re-layouts  3.48 us

profile of v2, /device:TPU:0, one launch (start us, length us, event | category | flops | bytes accessed | tf_op | source)
XLA Modules:
  0.0 81.7 jit_solution(15568201471112611753)
XLA Ops:
  0.0 0.0 copy-start
  0.0 1.0 %copy-done = bf16[4096,64]{0,1:T(8,128)(2,1)S(1)} copy-done((bf16[4096,64]{0,1:T(8,128)(2,1)S(1)}, bf16[4096,64]{0,1:T(8,128)(2,1)}, u32[]{:S(2)}) %copy-start) | copy-done | bytes 524312
  1.0 0.0 copy-start.1
  1.0 1.0 %copy-done.1 = bf16[512,512]{1,0:T(8,128)(2,1)S(1)} copy-done((bf16[512,512]{1,0:T(8,128)(2,1)S(1)}, bf16[512,512]{1,0:T(8,128)(2,1)}, u32[]{:S(2)}) %copy-start.1) | copy-done | bytes 524312
  2.1 0.0 copy-start.2
  2.1 0.7 copy-done.2
  2.8 0.0 copy-start.3
  2.8 0.7 copy-done.3
  3.5 73.7 %shard_map.46 = (f32[512,4096]{1,0:T(8,128)S(1)}, f32[16,8,256]{2,1,0:T(8,128)S(1)}, f32[8,512]{1,0:T(8,128)S(1)}) custom-call(bf16[64,4096]{1,0:T(8,128)(2,1)S(1)} %bitcast.5, bf16[512,512]{1,0:T(8,128)(2,1)S(1)} %copy-done.1, s32[1,512]{1,0:T(1,128)S(1)} %bitcast.7, s32[1,4096]{1,0:T(1,128)S(1)} %bitcast.6), custom_call_target="tpu_custom_call" | custom-call | tf_op jit(solution)/shard_map/pallas_call | solution.py:407
  77.2 4.5 %divide_select_fusion = f32[512,4096]{1,0:T(8,128)} fusion(f32[512,4096]{1,0:T(8,128)S(1)} %get-tuple-element.8, f32[4096]{0:T(1024)S(1)} %bitcast.8, f32[512]{0:T(512)S(1)} %bitcast.9, s32[4096]{0:T(1024)S(1)} %copy-done.2, s32[512]{0:T(512)S(1)} %copy-done.3), kind=kLoop, calls=%fused_computation | loop fusion | flops 10485760 | bytes 16814080 | tf_op jit(solution)/shard_map/jit(_where)/select_n | solution.py:454
  (2 shorter events, 0.0 us)
Async XLA Ops:
  0.0 1.0 %copy-start = (bf16[4096,64]{0,1:T(8,128)(2,1)S(1)}, bf16[4096,64]{0,1:T(8,128)(2,1)}, u32[]{:S(2)}) copy-start(bf16[4096,64]{0,1:T(8,128)(2,1)} %param.5) | copy-start | bytes 1572868
  1.0 1.0 %copy-start.1 = (bf16[512,512]{1,0:T(8,128)(2,1)S(1)}, bf16[512,512]{1,0:T(8,128)(2,1)}, u32[]{:S(2)}) copy-start(bf16[512,512]{1,0:T(8,128)(2,1)} %a_ref.1) | copy-start | bytes 1572868
  2.1 0.7 copy-start.2
  2.8 0.7 copy-start.3
